TPU v7x, 32 devices: a whole 2x2x4 slice. The times are simulated.
32 devices in a mesh: grp: 4 (over x, core), dp: 8 (over z, y).
Axes of the slice: x: 2, y: 2, z: 4, core: 2. Of those that a mesh axis runs over, the one named last changes fastest.
Arguments:
- query: bfloat16 [8, 512, 2560], P('dp', 'grp'), may hold values from -30 to 30
- resp_kv: bfloat16 [8, 512, 1024], P('dp', 'grp'), may hold values from -6 to 6
- prefix_kv: bfloat16 [8, 64, 1024], P('dp', 'grp'), may hold values from -30 to 30
- query_bias: float32 [2560], replicated, may hold values from -3 to 3
- kv_bias: float32 [1024], replicated, may hold values from -3 to 3
- out_grad: bfloat16 [8, 512, 2560], P('dp', 'grp'), may hold values from -6 to 6
- lengths: int32 [8, 4], P('dp', 'grp'), may hold values from 32 to 128
Outputs:
- attended: bfloat16 [8, 512, 2560], P('dp', 'grp')
- query_grad: bfloat16 [8, 512, 2560], P('dp', 'grp')
- resp_kv_grad: bfloat16 [8, 512, 1024], P('dp', 'grp')
- prefix_kv_grad: bfloat16 [8, 64, 1024], P('dp', 'grp')
- query_bias_grad: float32 [2560], replicated
- kv_bias_grad: float32 [1024], replicated
All inputs are finite; a program needn't handle non-finite values.
Results may differ from a plain program's by a relative error of at most 0.013.
The roundings to bfloat16 on the way count: a program that leaves them out, or rounds other values in their place, can miss the bound.
Values may be sent and summed in bfloat16 or wider, within the bound.
A program may use at most 64 MiB of HBM per device.

v0:
```python
import jax
import jax.numpy as jnp
from jax import lax
from jax.sharding import PartitionSpec as P

QH = 20
KVH = 4
HD = 128
NEG_BIG = -1e30


def attend_group(queries, cotangent, key_blocks, value_blocks, allows):
    factor = queries.shape[-1] ** (-0.5)
    scores = []
    for keys, allow in zip(key_blocks, allows):
        raw = jnp.einsum("thd,sd->hts", queries, keys, preferred_element_type=jnp.float32) * factor
        scores.append(jnp.where(allow[None], raw, NEG_BIG))
    highest = jnp.max(scores[0], -1, keepdims=True)
    for item in scores[1:]:
        highest = jnp.maximum(highest, jnp.max(item, -1, keepdims=True))
    powers = [jnp.exp(item - highest) for item in scores]
    totals = sum((jnp.sum(item, -1, keepdims=True) for item in powers))
    chances = [item / totals for item in powers]
    rounded = [item.astype(jnp.bfloat16) for item in chances]
    output = sum(
        (
            jnp.einsum("hts,sd->thd", wts, vals, preferred_element_type=jnp.float32)
            for wts, vals in zip(rounded, value_blocks)
        )
    )
    slopes = [
        jnp.einsum("thd,sd->hts", cotangent, vals, preferred_element_type=jnp.float32)
        for vals in value_blocks
    ]
    row_dot = sum(
        (jnp.sum(prob * slope, -1, keepdims=True) for prob, slope in zip(chances, slopes))
    )
    shifted = [
        (prob * (slope - row_dot)).astype(jnp.bfloat16) for prob, slope in zip(chances, slopes)
    ]
    query_grad = (
        sum(
            (
                jnp.einsum("hts,sd->thd", dsb, keys, preferred_element_type=jnp.float32)
                for dsb, keys in zip(shifted, key_blocks)
            )
        )
        * factor
    )
    key_grads = [
        jnp.einsum("hts,thd->sd", dsb, queries, preferred_element_type=jnp.float32) * factor
        for dsb in shifted
    ]
    value_grads = [
        jnp.einsum("hts,thd->sd", wts, cotangent, preferred_element_type=jnp.float32)
        for wts in rounded
    ]
    return (output, query_grad, key_grads, value_grads, shifted, rounded)


def local(query, resp_kv, prefix_kv, query_bias, kv_bias, out_grad, lengths):
    group = QH // KVH
    width = KVH * HD
    factor = HD ** (-0.5)
    prefix_own = (prefix_kv[0].astype(jnp.float32) + kv_bias).astype(jnp.bfloat16)
    own_rows = prefix_own.shape[0]
    prefix = lax.all_gather(prefix_own, "grp", axis=0, tiled=True)
    slots = query.shape[1]
    pre_rows = prefix.shape[0]
    length = lengths[0, 0]
    biased_query = (query[0].astype(jnp.float32) + query_bias).astype(jnp.bfloat16)
    own_kv = (resp_kv[0].astype(jnp.float32) + kv_bias).astype(jnp.bfloat16)
    position = jnp.arange(slots, dtype=jnp.int32)
    live = position < length
    grad_live = jnp.where(live[:, None], out_grad[0], jnp.zeros_like(out_grad[0]))
    allow_own = position[None, :] <= position[:, None]
    allow_pre = jnp.ones((slots, pre_rows), dtype=bool)
    queries = biased_query.reshape(slots, KVH, group, HD).transpose(1, 0, 2, 3)
    grads = grad_live.reshape(slots, KVH, group, HD).transpose(1, 0, 2, 3)
    pre_keys = prefix[:, :width].reshape(pre_rows, KVH, HD).transpose(1, 0, 2)
    pre_vals = prefix[:, width:].reshape(pre_rows, KVH, HD).transpose(1, 0, 2)
    own_keys = own_kv[:, :width].reshape(slots, KVH, HD).transpose(1, 0, 2)
    own_vals = own_kv[:, width:].reshape(slots, KVH, HD).transpose(1, 0, 2)

    def per_group(pieces):
        qpart, gpart, pkey, pval, okey, oval = pieces
        output, qgrad, kgrads, vgrads, shifted, rounded = attend_group(
            qpart,
            gpart,
            [jnp.concatenate([pkey, okey], 0)],
            [jnp.concatenate([pval, oval], 0)],
            [jnp.concatenate([allow_pre, allow_own], 1)],
        )
        return (
            output,
            qgrad,
            kgrads[0][:pre_rows],
            vgrads[0][:pre_rows],
            kgrads[0][pre_rows:],
            vgrads[0][pre_rows:],
            shifted[0][:, :, :pre_rows],
            rounded[0][:, :, :pre_rows],
        )

    output, qgrad, pk_grad, pv_grad, ok_grad, ov_grad, pre_shift, pre_prob = lax.map(
        per_group, (queries, grads, pre_keys, pre_vals, own_keys, own_vals)
    )
    output = output.transpose(1, 0, 2, 3).reshape(slots, QH * HD)
    attended = jnp.where(live[:, None], output, 0.0).astype(jnp.bfloat16)
    qgrad = qgrad.transpose(1, 0, 2, 3).reshape(slots, QH * HD)
    own_grad = jnp.concatenate(
        [
            ok_grad.transpose(1, 0, 2).reshape(slots, width),
            ov_grad.transpose(1, 0, 2).reshape(slots, width),
        ],
        -1,
    )
    shift_sum = jnp.sum(pre_shift.astype(jnp.float32), -1)
    prob_sum = jnp.sum(pre_prob.astype(jnp.float32), -1)
    key_total = jnp.einsum("jht,jthd->jd", shift_sum, queries.astype(jnp.float32)) * factor
    value_total = jnp.einsum("jht,jthd->jd", prob_sum, grads.astype(jnp.float32))
    pre_total = jnp.concatenate([key_total.reshape(width), value_total.reshape(width)], -1)
    count = lax.axis_size("grp") * own_rows
    shift_part = lax.slice_in_dim(pre_shift, 0, count, axis=3)
    prob_part = lax.slice_in_dim(pre_prob, 0, count, axis=3)
    key_part = (
        jnp.einsum("jhts,jthd->sjd", shift_part, queries, preferred_element_type=jnp.float32)
        * factor
    )
    value_part = jnp.einsum("jhts,jthd->sjd", prob_part, grads, preferred_element_type=jnp.float32)
    prefix_grad = lax.psum_scatter(
        jnp.concatenate(
            [key_part.reshape(count, width), value_part.reshape(count, width)], -1
        ).astype(jnp.bfloat16),
        "grp",
        scatter_dimension=0,
        tiled=True,
    )
    qsum, kvsum = lax.psum((jnp.sum(qgrad, 0), jnp.sum(own_grad, 0) + pre_total), ("grp", "dp"))
    return (
        attended[None],
        qgrad.astype(jnp.bfloat16)[None],
        own_grad.astype(jnp.bfloat16)[None],
        prefix_grad[None],
        qsum,
        kvsum,
    )


def solution(mesh):
    return jax.shard_map(
        local,
        mesh=mesh,
        in_specs=(
            P("dp", "grp", None),
            P("dp", "grp", None),
            P("dp", "grp", None),
            P(),
            P(),
            P("dp", "grp", None),
            P("dp", "grp"),
        ),
        out_specs=(
            P("dp", "grp", None),
            P("dp", "grp", None),
            P("dp", "grp", None),
            P("dp", "grp", None),
            P(),
            P(),
        ),
        check_vma=False,
    )
```

profile of v0, /device:TPU:0, one launch (start us, length us, event | category | flops | bytes accessed | tf_op | source)
XLA Modules:
  0.0 98.3 jit_solution(17740030026731421601)
XLA Ops:
  8.0 0.8 add.43
  8.7 0.8 fusion.49
  9.5 6.5 %all_gather.3 = bf16[64,1024]{1,0:T(8,128)(2,1)S(1)} all-gather(bf16[16,1024]{1,0:T(8,128)(2,1)S(1)} %fusion.49), channel_id=1, replica_groups=mesh['grp'=4,'dp'=8] {'grp'}, dimensions={0}, use_global_device_ids=true | all-gather | bytes 163840 | tf_op jit(solution)/shard_map/all_gather | solution.py:67
  16.7 1.1 %copy.17 = bf16[1,128,1024]{1,2,0:T(8,128)(2,1)S(1)} copy(bf16[1,128,1024]{2,1,0:T(8,128)(2,1)} %param.10) | data formatting | bytes 524288 | tf_op args[1]
  20.0 22.9 %while.21 = (s32[]{:T(128)}, bf16[4,128,5,128]{1,3,2,0:T(8,128)(2,1)}, f32[4,128,5,128]{1,3,2,0:T(8,128)}, f32[4,128,128]{1,2,0:T(8,128)}, f32[4,128,128]{1,2,0:...) while((s32[]{:T(128)}, ...), condition=%wide.region_4.5_spmd.clone, body=%wide.region_0.4_spmd.clone.sunk | while | flops 190725696 | bytes 7174342 | solution.py:105
  20.0 0.7 dynamic-slice_bitcast_fusion.5
  20.9 0.8 constant_dynamic-slice_fusion.5
  23.9 0.9 fusion.89
  24.8 1.0 fusion.90
  25.7 0.7 dynamic-slice_bitcast_fusion.5
  26.6 0.8 constant_dynamic-slice_fusion.5
  29.6 0.9 fusion.89
  30.5 1.0 fusion.90
  32.3 0.8 constant_dynamic-slice_fusion.5
  35.3 0.9 fusion.89
  36.2 1.0 fusion.90
  38.1 0.8 constant_dynamic-slice_fusion.5
  41.0 0.9 fusion.89
  41.9 1.0 fusion.90
  45.0 0.8 copy-done.2
  46.3 1.1 %copy.34 = bf16[1,128,2560]{2,1,0:T(8,128)(2,1)} copy(bf16[1,128,2560]{1,2,0:T(8,128)(2,1)S(1)} %select_convert_fusion) | data formatting | bytes 1310720
  47.4 1.1 %copy.35 = bf16[1,128,2560]{2,1,0:T(8,128)(2,1)} copy(bf16[1,128,2560]{1,2,0:T(8,128)(2,1)S(1)} %bitcast.229) | data formatting | bytes 1310720
  49.7 41.1 %all-reduce.1 = (f32[2560]{0:T(1024)}, f32[1024]{0:T(1024)}) all-reduce(f32[2560]{0:T(1024)S(1)} %reduce_sum.57, f32[1024]{0:T(1024)S(1)} %maximum_add_fusion), channel_id=1, replica_groups=mesh['grp'=4,'dp'=8] {'grp','dp'}, use_global_device_ids=true, to_apply=%region_7.8 | all-reduce | flops 3584 | bytes 28672 | tf_op jit(solution)/shard_map/psum | solution.py:139
  90.7 0.7 pad_maximum_fusion
  (132 shorter events, 17.0 us)
Async XLA Ops:
  7.2 10.7 %copy-start.9 = (f32[1024]{0:T(1024)S(1)}, f32[1024]{0:T(1024)}, u32[]{:S(2)}) copy-start(f32[1024]{0:T(1024)} %param.13) | copy-start | bytes 12292
  7.2 84.3 %reduce-scatter.2.cloned.1.call-start = ((), (), s32[]{:S(2)}) async-start(), calls=%async_computation.1 | async-start | bytes 163840 | tf_op jit(solution)/shard_map/reduce_scatter | solution.py:131
  7.9 12.0 %copy-start.10 = (pred[128]{0:T(512)(128)(4,1)}, pred[128]{0:T(512)(128)(4,1)S(1)}, u32[]{:S(2)}) copy-start(pred[128]{0:T(512)(128)(4,1)S(1)} %iota_compare_fusion.1) | copy-start | bytes 388
  8.0 10.8 %copy-start.6 = (bf16[1,128,2560]{2,1,0:T(8,128)(2,1)S(1)}, bf16[1,128,2560]{2,1,0:T(8,128)(2,1)}, u32[]{:S(2)}) copy-start(bf16[1,128,2560]{2,1,0:T(8,128)(2,1)} %param.9) | copy-start | bytes 1966084
  18.1 1.1 %copy-start.7 = (bf16[1,128,2560]{2,1,0:T(8,128)(2,1)S(1)}, bf16[1,128,2560]{2,1,0:T(8,128)(2,1)}, u32[]{:S(2)}) copy-start(bf16[1,128,2560]{2,1,0:T(8,128)(2,1)} %param.14) | copy-start | bytes 1966084
  42.9 1.5 %copy-start.1 = (bf16[4,5,128,64]{2,3,1,0:T(8,128)(2,1)}, bf16[4,5,128,64]{2,3,1,0:T(8,128)(2,1)S(1)}, u32[]{:S(2)}) copy-start(bf16[4,5,128,64]{2,3,1,0:T(8,128)(2,1)S(1)} %get-tuple-element.88) | copy-start | bytes 983044
  42.9 1.5 %copy-start.3 = (bf16[4,5,128,64]{2,3,1,0:T(8,128)(2,1)}, bf16[4,5,128,64]{2,3,1,0:T(8,128)(2,1)S(1)}, u32[]{:S(2)}) copy-start(bf16[4,5,128,64]{2,3,1,0:T(8,128)(2,1)S(1)} %get-tuple-element.87) | copy-start | bytes 983044
  42.9 1.6 %copy-start = (f32[4,128,5,128]{1,3,2,0:T(8,128)S(1)}, f32[4,128,5,128]{1,3,2,0:T(8,128)}, u32[]{:S(2)}) copy-start(f32[4,128,5,128]{1,3,2,0:T(8,128)} %get-tuple-element.84) | copy-start | bytes 3932164
  44.9 1.0 copy-start.2
  44.9 1.1 %copy-start.4 = (bf16[4,5,128,64]{2,3,1,0:T(8,128)(2,1)S(1)}, bf16[4,5,128,64]{2,3,1,0:T(8,128)(2,1)}, u32[]{:S(2)}) copy-start(bf16[4,5,128,64]{2,3,1,0:T(8,128)(2,1)} %copy-done.3) | copy-start | bytes 983044
  44.9 1.3 %copy-start.8 = (bf16[4,128,5,128]{1,3,2,0:T(8,128)(2,1)S(1)}, bf16[4,128,5,128]{1,3,2,0:T(8,128)(2,1)}, u32[]{:S(2)}) copy-start(bf16[4,128,5,128]{1,3,2,0:T(8,128)(2,1)} %get-tuple-element.83) | copy-start | bytes 1966084
  44.9 1.3 %copy-start.11 = (pred[128]{0:T(512)(128)(4,1)S(1)}, pred[128]{0:T(512)(128)(4,1)}, u32[]{:S(2)}) copy-start(pred[128]{0:T(512)(128)(4,1)} %copy-done.10) | copy-start | bytes 388
  47.4 1.7 %copy-start.5 = (f32[4,128,128]{1,2,0:T(8,128)S(1)}, f32[4,128,128]{1,2,0:T(8,128)}, u32[]{:S(2)}) copy-start(f32[4,128,128]{1,2,0:T(8,128)} %get-tuple-element.85) | copy-start | bytes 786436
Sparse Core Ops, SparseCore 0:
  44.5 21.3 reduce-scatter.1
where the time goes:
time: 99.2 us; the launch traced here: 98.3 us
  blocking collectives  47.6 us (48%)
  local copies, waits for them, and re-layouts  17.9 us (18%)
  between operations  15 us (15%)
  matrix products  13 us (13%)
  other arithmetic  4.4 us (4%)
    psum x1, blocking collectives, local(): lax.psum((jnp.sum(qgrad, 0), jnp.sum(own_grad, 0) + pre_total), ('grp', '...  41.1 us
    all_gather x1, blocking collectives, local(): prefix = lax.all_gather(prefix_own, 'grp', axis=0, tiled=True)  6.51 us
    unnamed x31, local copies, waits for them, and re-layouts  5.78 us
    dynamic_slice x16, local copies, waits for them, and re-layouts, local(): lax.map(per_group, (queries, grads, pre_keys, pre_vals, own_keys, own_vals))  4.02 us
    dot_general x4, matrix products, attend_group(): jnp.einsum('hts,sd->thd', dsb, keys, preferred_element_type=jnp.float32)  3.86 us
    dot_general x4, matrix products, attend_group(): jnp.einsum('hts,sd->thd', wts, vals, preferred_element_type=jnp.float32)  3.6 us
    dynamic_update_slice x16, local copies, waits for them, and re-layouts, local(): lax.map(per_group, (queries, grads, pre_keys, pre_vals, own_keys, own_vals))  3.37 us
    squeeze x8, local copies, waits for them, and re-layouts, local(): lax.map(per_group, (queries, grads, pre_keys, pre_vals, own_keys, own_vals))  2.9 us
  transfers between devices with their start and end apart: 1, of which 0 were waited for; matrix products, arithmetic and copies ran while one was open for 5% of the time, Pallas kernels for 0%

commit v1 on v0

--- a/solution.py
+++ b/solution.py
@@ -136,7 +136,9 @@
         scatter_dimension=0,
         tiled=True,
     )
-    qsum, kvsum = lax.psum((jnp.sum(qgrad, 0), jnp.sum(own_grad, 0) + pre_total), ("grp", "dp"))
+    qsum, kvsum = lax.psum(
+        lax.psum((jnp.sum(qgrad, 0), jnp.sum(own_grad, 0) + pre_total), "dp"), "grp"
+    )
     return (
         attended[None],
         qgrad.astype(jnp.bfloat16)[None],

time: 99.2 us -> 107 us (1.079)
  blocking collectives: 47.6 us -> 55 us
    psum x1 -> x2, blocking collectives: 41.1 us -> 48.5 us  [the longest x1 37.8 us: local(): lax.psum((jnp.sum(qgrad, 0), jnp.sum(own_grad, 0) + pre_total), 'dp')]
where the time goes in v1:
time: 107 us; the launch traced here: 106 us
  blocking collectives  55 us (51%)
  local copies, waits for them, and re-layouts  17.9 us (17%)
  between operations  15 us (14%)
  matrix products  13 us (12%)
  other arithmetic  4.4 us (4%)
    psum x1, blocking collectives, local(): lax.psum((jnp.sum(qgrad, 0), jnp.sum(own_grad, 0) + pre_total), 'dp')  37.8 us
    psum x1, blocking collectives, local(): lax.psum(lax.psum((jnp.sum(qgrad, 0), jnp.sum(own_grad, 0) + pre_total),...  10.7 us
    all_gather x1, blocking collectives, local(): prefix = lax.all_gather(prefix_own, 'grp', axis=0, tiled=True)  6.51 us
    unnamed x31, local copies, waits for them, and re-layouts  5.78 us
    dynamic_slice x16, local copies, waits for them, and re-layouts, local(): lax.map(per_group, (queries, grads, pre_keys, pre_vals, own_keys, own_vals))  4.02 us
    dot_general x4, matrix products, attend_group(): jnp.einsum('hts,sd->thd', dsb, keys, preferred_element_type=jnp.float32)  3.86 us
    dot_general x4, matrix products, attend_group(): jnp.einsum('hts,sd->thd', wts, vals, preferred_element_type=jnp.float32)  3.6 us
    dynamic_update_slice x16, local copies, waits for them, and re-layouts, local(): lax.map(per_group, (queries, grads, pre_keys, pre_vals, own_keys, own_vals))  3.37 us
  transfers between devices with their start and end apart: 1, of which 0 were waited for; matrix products, arithmetic and copies ran while one was open for 5% of the time, Pallas kernels for 0%

profile of v1, /device:TPU:0, one launch (start us, length us, event | category | flops | bytes accessed | tf_op | source)
XLA Modules:
  0.0 105.7 jit_solution(16916503548243414948)
XLA Ops:
  8.0 0.8 add.47
  8.7 0.8 fusion.49
  9.5 6.5 %all_gather.3 = bf16[64,1024]{1,0:T(8,128)(2,1)S(1)} all-gather(bf16[16,1024]{1,0:T(8,128)(2,1)S(1)} %fusion.49), channel_id=1, replica_groups=mesh['grp'=4,'dp'=8] {'grp'}, dimensions={0}, use_global_device_ids=true | all-gather | bytes 163840 | tf_op jit(solution)/shard_map/all_gather | solution.py:67
  16.7 1.1 %copy.17 = bf16[1,128,1024]{1,2,0:T(8,128)(2,1)S(1)} copy(bf16[1,128,1024]{2,1,0:T(8,128)(2,1)} %param.10) | data formatting | bytes 524288 | tf_op args[1]
  20.0 22.9 %while.21 = (s32[]{:T(128)}, bf16[4,128,5,128]{1,3,2,0:T(8,128)(2,1)}, f32[4,128,5,128]{1,3,2,0:T(8,128)}, f32[4,128,128]{1,2,0:T(8,128)}, f32[4,128,128]{1,2,0:...) while((s32[]{:T(128)}, ...), condition=%wide.region_4.5_spmd.clone, body=%wide.region_0.4_spmd.clone.sunk | while | flops 190725696 | bytes 7174342 | solution.py:105
  20.0 0.7 dynamic-slice_bitcast_fusion.5
  20.9 0.8 constant_dynamic-slice_fusion.5
  23.9 0.9 fusion.89
  24.8 1.0 fusion.90
  26.6 0.8 constant_dynamic-slice_fusion.5
  29.6 0.9 fusion.89
  30.5 1.0 fusion.90
  32.3 0.8 constant_dynamic-slice_fusion.5
  35.3 0.9 fusion.89
  36.2 1.0 fusion.90
  38.1 0.8 constant_dynamic-slice_fusion.5
  41.0 0.9 fusion.89
  41.9 1.0 fusion.90
  45.0 0.8 copy-done.2
  46.3 1.1 %copy.34 = bf16[1,128,2560]{2,1,0:T(8,128)(2,1)} copy(bf16[1,128,2560]{1,2,0:T(8,128)(2,1)S(1)} %select_convert_fusion) | data formatting | bytes 1310720
  47.4 1.1 %copy.35 = bf16[1,128,2560]{2,1,0:T(8,128)(2,1)} copy(bf16[1,128,2560]{1,2,0:T(8,128)(2,1)S(1)} %bitcast.229) | data formatting | bytes 1310720
  49.7 37.8 %all-reduce.1 = (f32[2560]{0:T(1024)S(1)}, f32[1024]{0:T(1024)S(1)}) all-reduce(f32[2560]{0:T(1024)S(1)} %reduce_sum.57, f32[1024]{0:T(1024)S(1)} %maximum_add_fusion), channel_id=1, replica_groups=mesh['grp'=4,'dp'=8] {'dp'}, use_global_device_ids=true, to_apply=%region_7.8 | all-reduce | flops 3584 | bytes 28672 | tf_op jit(solution)/shard_map/psum | solution.py:140
  87.4 10.7 %all-reduce.2 = (f32[2560]{0:T(1024)}, f32[1024]{0:T(1024)}) all-reduce(f32[2560]{0:T(1024)S(1)} %get-tuple-element.162, f32[1024]{0:T(1024)S(1)} %get-tuple-element.163), channel_id=1, replica_groups=mesh['grp'=4,'dp'=8] {'grp'}, use_global_device_ids=true, to_apply=%region_8.9 | all-reduce | flops 3584 | bytes 28672 | tf_op jit(solution)/shard_map/psum | solution.py:139
  98.2 0.7 pad_maximum_fusion
  (133 shorter events, 17.7 us)
Async XLA Ops:
  7.2 10.7 %copy-start.9 = (f32[1024]{0:T(1024)S(1)}, f32[1024]{0:T(1024)}, u32[]{:S(2)}) copy-start(f32[1024]{0:T(1024)} %param.13) | copy-start | bytes 12292
  7.2 91.7 %reduce-scatter.2.cloned.1.call-start = ((), (), s32[]{:S(2)}) async-start(), calls=%async_computation.1 | async-start | bytes 163840 | tf_op jit(solution)/shard_map/reduce_scatter | solution.py:131
  7.9 12.0 %copy-start.10 = (pred[128]{0:T(512)(128)(4,1)}, pred[128]{0:T(512)(128)(4,1)S(1)}, u32[]{:S(2)}) copy-start(pred[128]{0:T(512)(128)(4,1)S(1)} %iota_compare_fusion.1) | copy-start | bytes 388
  8.0 10.8 %copy-start.6 = (bf16[1,128,2560]{2,1,0:T(8,128)(2,1)S(1)}, bf16[1,128,2560]{2,1,0:T(8,128)(2,1)}, u32[]{:S(2)}) copy-start(bf16[1,128,2560]{2,1,0:T(8,128)(2,1)} %param.9) | copy-start | bytes 1966084
  18.1 1.1 %copy-start.7 = (bf16[1,128,2560]{2,1,0:T(8,128)(2,1)S(1)}, bf16[1,128,2560]{2,1,0:T(8,128)(2,1)}, u32[]{:S(2)}) copy-start(bf16[1,128,2560]{2,1,0:T(8,128)(2,1)} %param.14) | copy-start | bytes 1966084
  42.9 1.5 %copy-start.1 = (bf16[4,5,128,64]{2,3,1,0:T(8,128)(2,1)}, bf16[4,5,128,64]{2,3,1,0:T(8,128)(2,1)S(1)}, u32[]{:S(2)}) copy-start(bf16[4,5,128,64]{2,3,1,0:T(8,128)(2,1)S(1)} %get-tuple-element.88) | copy-start | bytes 983044
  42.9 1.5 %copy-start.3 = (bf16[4,5,128,64]{2,3,1,0:T(8,128)(2,1)}, bf16[4,5,128,64]{2,3,1,0:T(8,128)(2,1)S(1)}, u32[]{:S(2)}) copy-start(bf16[4,5,128,64]{2,3,1,0:T(8,128)(2,1)S(1)} %get-tuple-element.87) | copy-start | bytes 983044
  42.9 1.6 %copy-start = (f32[4,128,5,128]{1,3,2,0:T(8,128)S(1)}, f32[4,128,5,128]{1,3,2,0:T(8,128)}, u32[]{:S(2)}) copy-start(f32[4,128,5,128]{1,3,2,0:T(8,128)} %get-tuple-element.84) | copy-start | bytes 3932164
  44.9 1.0 copy-start.2
  44.9 1.1 %copy-start.4 = (bf16[4,5,128,64]{2,3,1,0:T(8,128)(2,1)S(1)}, bf16[4,5,128,64]{2,3,1,0:T(8,128)(2,1)}, u32[]{:S(2)}) copy-start(bf16[4,5,128,64]{2,3,1,0:T(8,128)(2,1)} %copy-done.3) | copy-start | bytes 983044
  44.9 1.3 %copy-start.8 = (bf16[4,128,5,128]{1,3,2,0:T(8,128)(2,1)S(1)}, bf16[4,128,5,128]{1,3,2,0:T(8,128)(2,1)}, u32[]{:S(2)}) copy-start(bf16[4,128,5,128]{1,3,2,0:T(8,128)(2,1)} %get-tuple-element.83) | copy-start | bytes 1966084
  44.9 1.3 %copy-start.11 = (pred[128]{0:T(512)(128)(4,1)S(1)}, pred[128]{0:T(512)(128)(4,1)}, u32[]{:S(2)}) copy-start(pred[128]{0:T(512)(128)(4,1)} %copy-done.10) | copy-start | bytes 388
  47.4 1.7 %copy-start.5 = (f32[4,128,128]{1,2,0:T(8,128)S(1)}, f32[4,128,128]{1,2,0:T(8,128)}, u32[]{:S(2)}) copy-start(f32[4,128,128]{1,2,0:T(8,128)} %get-tuple-element.85) | copy-start | bytes 786436
Sparse Core Ops, SparseCore 0:
  44.5 21.2 reduce-scatter.1
